TPU v7x, 32 devices: a whole 2x2x4 slice. The times are simulated.
32 devices in a mesh: row: 4 (over y, x), col: 2 (over core), head: 4 (over z).
Axes of the slice: x: 2, y: 2, z: 4, core: 2. Of those that a mesh axis runs over, the one named last changes fastest.
Arguments:
- queries: bfloat16 [192, 64, 1024], P('row', 'col', 'head'), may hold values from -16 to 16
- keys: bfloat16 [192, 64, 1024], P('row', 'col', 'head'), may hold values from -16 to 16
- values: bfloat16 [192, 64, 1024], P('row', 'col', 'head'), may hold values from -16 to 16
- positions: int32 [2, 192, 64], P(None, 'row', 'col'), may hold values from 0 to 192, as said below
- conv_weight: float32 [9, 1024], P(None, 'head'), may hold values from -2 to 2
- norm_gain: float32 [1024], P('head'), may hold values from 0.5 to 1.5
- norm_bias: float32 [1024], P('head'), may hold values from -3 to 3
Outputs:
- normed: bfloat16 [192, 64, 1024], P('row', 'col', 'head')
Inputs may be any that keep to these rules, and one draw needn't show every extreme that they name: positions[0] depends only on the grid row and positions[1] only on the grid column; each starts at 0 on the first grid line, rises by 0, 1 or 2 from one line to the next, and ends at 192 (rows) or 64 (columns).
All inputs are finite; a program needn't handle non-finite values.
Results may differ from a plain program's by a relative error of at most 0.0055.
Values may be sent and summed in bfloat16 or wider, within the bound.
A program may use at most 128 MiB of HBM per device.

v0:
```python
import functools
import math

import jax
import jax.numpy as jnp
from jax import lax
from jax.experimental import pallas as pl
from jax.experimental.pallas import tpu as pltpu
from jax.sharding import PartitionSpec as P

HD = 64
D = 1024
AGR = 4
EPS = 1e-05
F32 = jnp.float32
BF16 = jnp.bfloat16
MESH = pl.DeviceIdType.MESH
NT = (((1,), (1,)), ((), ()))
TN = (((0,), (0,)), ((), ()))


def iota(shape, dim):
    return lax.broadcasted_iota(jnp.int32, shape, dim)


def kernel(
    n_row, n_col, n_head,
    q_hbm, k_hbm, v_hbm, pos_hbm, w_hbm,
    conv, stat_ref,
    pos_ref, w_ref, q_in, k_in, vp, lh, rh, qt, kt, tabs, tabr, ag, s_ref, pt, mb, sb, hb, own,
    in_sem, ag_s, ag_r, mb_s, mb_r, sb_s, sb_r, hb_s, hb_r, halo_s, halo_r,
):
    rows, cols, chan = q_in.shape
    heads = chan // HD
    patches = rows * cols
    tiles = n_row * n_col
    agents = tiles * AGR
    ha = agents * heads
    row, col, head = lax.axis_index("row"), lax.axis_index("col"), lax.axis_index("head")
    me = row * n_col + col

    def peer(o):
        t = lax.rem(me + o, tiles)
        return (t // n_col, lax.rem(t, n_col), head)

    def head_peer(o):
        return (row, col, lax.rem(head + o, n_head))

    def everyone(ref, send, recv):
        some = ref.at[pl.ds(0, tiles - 1)]
        return pltpu.make_async_remote_copy(
            some, some, send, recv, device_id=peer(1), device_id_type=MESH
        )

    loads = [
        pltpu.make_async_copy(pos_hbm, pos_ref, in_sem.at[3]),
        pltpu.make_async_copy(q_hbm, q_in, in_sem.at[0]),
        pltpu.make_async_copy(k_hbm, k_in, in_sem.at[1]),
        pltpu.make_async_copy(v_hbm, vp.at[pl.ds(1, rows)], in_sem.at[2]),
        pltpu.make_async_copy(w_hbm, w_ref, in_sem.at[4]),
    ]
    for c in loads:
        c.start()

    barrier = pltpu.get_barrier_semaphore()
    for o in range(1, tiles):
        pl.semaphore_signal(barrier, inc=1, device_id=peer(o), device_id_type=MESH)
    for o in range(1, n_head):
        pl.semaphore_signal(barrier, inc=1, device_id=head_peer(o), device_id_type=MESH)

    lane = iota((1, chan), 1)
    freq = jnp.zeros((1, chan), F32)
    for j in range(HD // 4):
        freq = jnp.where(lane % (HD // 4) == j, F32(100.0 ** (-j / (HD // 4))), freq)
    row_lane = (lane % HD) < HD // 2
    loads[0].wait()
    eye = iota((rows, rows), 0) == iota((rows, rows), 1)
    row_line = jnp.broadcast_to(pos_ref[0, 0:1, :].astype(F32), (rows, rows))
    row_pos = jnp.sum(jnp.where(eye, row_line, 0.0), axis=1, keepdims=True)
    col_pos = pos_ref[1, :, 0:1].astype(F32)
    row_ang = row_pos * freq
    col_ang = col_pos * freq
    tabr[0] = jnp.where(row_lane, jnp.cos(row_ang), 0.0)
    tabr[1] = jnp.where(row_lane, jnp.sin(row_ang), 0.0)
    tabs[0] = jnp.where(row_lane, 0.0, jnp.cos(col_ang))
    tabs[1] = jnp.where(row_lane, 0.0, jnp.sin(col_ang))
    src, dst = iota((chan, chan), 0), iota((chan, chan), 1)
    low = (dst % (HD // 2)) < HD // 4
    turn = jnp.where(low & (src - dst == HD // 4), -1.0, 0.0) + jnp.where(
        jnp.logical_not(low) & (dst - src == HD // 4), 1.0, 0.0
    )
    turn = turn.astype(BF16)

    step = rows // AGR

    def rotate(ref, to, cell):
        x = ref[pl.ds(cell * step, step)].reshape(step * cols, chan)
        crossed = jnp.dot(x, turn, preferred_element_type=F32).reshape(step, cols, chan)
        x = x.astype(F32).reshape(step, cols, chan)
        cosine = tabr[0, pl.ds(cell * step, step)][:, None, :] + tabs[0][None]
        sine = tabr[1, pl.ds(cell * step, step)][:, None, :] + tabs[1][None]
        y = (x * cosine + crossed * sine).astype(BF16)
        to[pl.ds(cell * step * cols, step * cols)] = y.reshape(step * cols, chan)
        return y

    loads[1].wait()
    block = []
    for cell in range(AGR):
        y = rotate(q_in, qt, cell)
        total = jnp.sum(y.astype(F32).reshape(step * cols, chan), axis=0, keepdims=True)
        block.append((total * (1.0 / (step * cols))).astype(BF16).astype(F32))
    block = jnp.concatenate(block, axis=0) * (1.0 / math.sqrt(HD))
    ag[me] = block.astype(BF16)

    pl.semaphore_wait(barrier, tiles - 1 + n_head - 1)
    ag_copies = [
        pltpu.make_async_remote_copy(
            ag.at[me], ag.at[me], ag_s, ag_r, device_id=peer(o), device_id_type=MESH
        )
        for o in range(1, tiles)
    ]
    for c in ag_copies:
        c.start()

    edge = 16
    halos = []
    spots = [(-1, 0), (1, 0), (0, -1), (0, 1), (-1, -1), (-1, 1), (1, -1), (1, 1)]
    for i, (dr, dc) in enumerate(spots):
        frm = v_hbm
        if dc == 0:
            frm = v_hbm.at[0 if dr < 0 else rows - 1]
            to = vp.at[rows + 1 if dr < 0 else 0]
        else:
            part = pl.ds(0, edge) if dc < 0 else pl.ds(cols - edge, edge)
            slab = rh if dc < 0 else lh
            if dr == 0:
                frm, to = v_hbm.at[:, part], slab.at[pl.ds(1, rows)]
            else:
                frm = v_hbm.at[0 if dr < 0 else rows - 1, part]
                to = slab.at[rows + 1 if dr < 0 else 0]
        exists = (row + dr >= 0) & (row + dr < n_row) & (col + dc >= 0) & (col + dc < n_col)
        comes = (row - dr >= 0) & (row - dr < n_row) & (col - dc >= 0) & (col - dc < n_col)
        target = (
            jnp.clip(row + dr, 0, n_row - 1), jnp.clip(col + dc, 0, n_col - 1), head,
        )
        c = pltpu.make_async_remote_copy(
            frm, to, halo_s.at[i], halo_r.at[i], device_id=target, device_id_type=MESH
        )
        halos.append((c, exists, comes))
        pl.when(exists)(c.start)

        @pl.when(jnp.logical_not(comes))
        def _():
            to[...] = jnp.zeros(to.shape, BF16)

    loads[2].wait()
    for cell in range(AGR):
        rotate(k_in, kt, cell)

    loads[3].wait()
    loads[4].wait()
    everyone(ag, ag_s, ag_r).wait()
    mask = (iota((ha, chan), 0) % heads) == iota((ha, chan), 1) // HD
    copies = (iota((ha, agents), 0) // heads == iota((ha, agents), 1)).astype(BF16)
    bd = jnp.dot(copies, ag[...].reshape(agents, chan), preferred_element_type=F32)
    bd = jnp.where(mask, bd, 0.0).astype(BF16)

    chunk = 256
    top = None
    for i in range(patches // chunk):
        s = lax.dot_general(bd, kt[pl.ds(i * chunk, chunk)], NT, preferred_element_type=F32)
        s_ref[:, pl.ds(i * chunk, chunk)] = s
        top = s if top is None else jnp.maximum(top, s)
    peak = jnp.max(top, axis=1, keepdims=True)
    sums = jnp.zeros((ha, chunk), F32)
    numer = jnp.zeros((ha, chan), F32)
    for i in range(patches // chunk):
        e = jnp.exp(s_ref[:, pl.ds(i * chunk, chunk)] - peak)
        sums = sums + e
        v = vp[pl.ds(1 + i * (chunk // cols), chunk // cols)].reshape(chunk, chan)
        numer = numer + jnp.dot(e.astype(BF16), v, preferred_element_type=F32)
    total = jnp.sum(sums, axis=1, keepdims=True)
    means = jnp.where(mask, numer / total, 0.0).astype(BF16)
    pick = (iota((agents, ha), 1) // heads == iota((agents, ha), 0)).astype(BF16)
    mb[me] = jnp.dot(pick, means, preferred_element_type=F32).astype(BF16)
    diag = iota((ha, ha), 0) == iota((ha, ha), 1)
    peak_row = jnp.sum(jnp.where(diag, peak, 0.0), axis=0, keepdims=True)
    total_row = jnp.sum(jnp.where(diag, total, 0.0), axis=0, keepdims=True)
    sb[me] = jnp.where(iota((8, ha), 0) == 0, peak_row, total_row)
    merge = []
    for o in range(1, tiles):
        merge.append(pltpu.make_async_remote_copy(
            sb.at[me], sb.at[me], sb_s, sb_r, device_id=peer(o), device_id_type=MESH
        ))
        merge.append(pltpu.make_async_remote_copy(
            mb.at[me], mb.at[me], mb_s, mb_r, device_id=peer(o), device_id_type=MESH
        ))
    for c in merge:
        c.start()

    for i in range(patches // chunk):
        s = lax.dot_general(bd, qt[pl.ds(i * chunk, chunk)], NT, preferred_element_type=F32)
        s = s.reshape(ha // 8, 8, chunk)
        m = jnp.max(s, axis=0)
        shift = heads
        while shift < 8:
            m = jnp.maximum(m, pltpu.roll(m, shift, 0))
            shift *= 2
        p = jnp.exp(s - m[None])
        z = jnp.sum(p, axis=0)
        shift = heads
        while shift < 8:
            z = z + pltpu.roll(z, shift, 0)
            shift *= 2
        p = (p * (1.0 / z)[None]).reshape(ha, chunk)
        pt[pl.ds(i * chunk, chunk)] = p.T.astype(BF16)

    for c, exists, comes in halos:
        pl.when(exists)(c.wait_send)
        pl.when(comes)(c.wait_recv)
    part = 2

    def conv_rows(i, _):
        r0 = i * part
        line = [vp[r0 + d].astype(F32) for d in range(part + 2)]
        left = [lh[r0 + d].astype(F32)[edge - 8:] for d in range(part + 2)]
        right = [rh[r0 + d].astype(F32)[:8] for d in range(part + 2)]
        for r in range(part):
            def taps(src, dj):
                acc = src[r] * w_ref[pl.ds(dj, 1)]
                acc = acc + src[r + 1] * w_ref[pl.ds(3 + dj, 1)]
                return acc + src[r + 2] * w_ref[pl.ds(6 + dj, 1)]
            first = jnp.concatenate([taps(left, 0), taps(line, 0)], axis=0)
            first = pltpu.roll(first, 1, 0)[8:]
            last = jnp.concatenate([taps(line, 2), taps(right, 2)], axis=0)
            last = pltpu.roll(last, cols + 7, 0)[:cols]
            conv[r0 + r] = first + taps(line, 1) + last
        return 0

    lax.fori_loop(0, rows // part, conv_rows, 0)

    everyone(sb, sb_s, sb_r).wait()
    everyone(mb, mb_s, mb_r).wait()
    st = sb[...]
    peaks, totals = st[:, 0, :], st[:, 1, :]
    best = jnp.max(peaks, axis=0, keepdims=True)
    weight = jnp.exp(peaks - best) * totals
    weight = weight / jnp.sum(weight, axis=0, keepdims=True)
    group = max(1, min(tiles, 256 // agents))
    spread = iota((group, agents, ha), 2) // heads == iota((group, agents, ha), 1)
    av = jnp.zeros((ha, chan), F32)
    for g in range(0, tiles, group):
        wide = jnp.where(spread, weight[g:g + group, None, :], 0.0).reshape(group * agents, ha)
        high = wide.astype(BF16)
        less = (wide - high.astype(F32)).astype(BF16)
        every = mb[g:g + group].reshape(group * agents, chan)
        av = av + lax.dot_general(high, every, TN, preferred_element_type=F32)
        av = av + lax.dot_general(less, every, TN, preferred_element_type=F32)
    av = jnp.where(mask, av, 0.0).astype(BF16)

    pieces = own.shape[0]
    size = patches // pieces
    blocks = size // 128
    lines = size // cols
    eye = iota((128, 128), 0) == iota((128, 128), 1)
    for p in range(pieces):
        x = jnp.dot(pt[pl.ds(p * size, size)], av, preferred_element_type=F32)
        x = x + conv[pl.ds(p * lines, lines)].reshape(size, chan)
        conv[pl.ds(p * lines, lines)] = x.reshape(lines, cols, chan)
        one = jnp.sum(x, axis=1, keepdims=True)
        two = jnp.sum(x * x, axis=1, keepdims=True)
        for j, what in enumerate((one, two)):
            for b in range(blocks):
                column = what[b * 128:(b + 1) * 128]
                own[p, pl.ds(j * blocks + b, 1)] = jnp.sum(
                    jnp.where(eye, column, 0.0), axis=0, keepdims=True
                )
        for o in range(1, n_head):
            pltpu.make_async_remote_copy(
                own.at[p], hb.at[p, o - 1], hb_s.at[p], hb_r.at[p],
                device_id=head_peer(o), device_id_type=MESH,
            ).start()

    for p in range(pieces):
        pltpu.make_async_remote_copy(
            hb.at[p], hb.at[p], hb_s.at[p], hb_r.at[p],
            device_id=head_peer(1), device_id_type=MESH,
        ).wait()
        t = own[p]
        for o in range(1, n_head):
            t = t + hb[p, o - 1]
        average = t[:blocks] * (1.0 / D)
        variance = t[blocks:] * (1.0 / D) - average * average
        stat_ref[p] = jnp.concatenate([average, lax.rsqrt(variance + EPS)], axis=0)


def normalize(x_ref, stat_ref, gain_ref, bias_ref, out_hbm, obuf, out_sem):
    rows, cols, chan = x_ref.shape
    pieces = stat_ref.shape[0]
    lines = rows // pieces
    blocks = lines * cols // 128
    part = 128 // cols
    gain, bias = gain_ref[...], bias_ref[...]
    outs = []
    for p in range(pieces):
        for b in range(blocks):
            a = jnp.broadcast_to(stat_ref[p, b:b + 1], (128, 128)).T
            g = jnp.broadcast_to(stat_ref[p, blocks + b:blocks + b + 1], (128, 128)).T
            a = jnp.concatenate([a] * (chan // 128), axis=1)
            g = jnp.concatenate([g] * (chan // 128), axis=1)
            at = pl.ds(p * lines + b * part, part)
            y = (x_ref[at].reshape(128, chan) - a) * g * gain + bias
            obuf[at] = y.astype(BF16).reshape(part, cols, chan)
        at = pl.ds(p * lines, lines)
        c = pltpu.make_async_copy(obuf.at[at], out_hbm.at[at], out_sem.at[p])
        c.start()
        outs.append(c)
    for c in outs:
        c.wait()


def shards(n_row, n_col, n_head, queries, keys, values, positions, conv_weight, gain, bias):
    rows, cols, chan = queries.shape
    heads = chan // HD
    tiles = n_row * n_col
    agents = tiles * AGR
    ha = agents * heads
    patches = rows * cols
    pieces = patches // 512
    need = min(56 * 1024 * 1024, 14 * 1024 * 1024 + 4 * ha * tiles * agents * 8)
    hbm = pl.BlockSpec(memory_space=pltpu.HBM)
    vmem = pl.BlockSpec(memory_space=pltpu.VMEM)
    dma = pltpu.SemaphoreType.DMA
    summed, stats = pl.pallas_call(
        functools.partial(kernel, n_row, n_col, n_head),
        out_shape=[pltpu.VMEM((rows, cols, chan), F32), pltpu.VMEM((pieces, 8, 128), F32)],
        in_specs=[hbm] * 5,
        out_specs=[vmem, vmem],
        scratch_shapes=[
            pltpu.VMEM((2, cols, rows), jnp.int32),
            pltpu.VMEM((9, chan), F32),
            pltpu.VMEM((rows, cols, chan), BF16),
            pltpu.VMEM((rows, cols, chan), BF16),
            pltpu.VMEM((rows + 2, cols, chan), BF16),
            pltpu.VMEM((rows + 2, 16, chan), BF16),
            pltpu.VMEM((rows + 2, 16, chan), BF16),
            pltpu.VMEM((patches, chan), BF16),
            pltpu.VMEM((patches, chan), BF16),
            pltpu.VMEM((2, cols, chan), F32),
            pltpu.VMEM((2, rows, chan), F32),
            pltpu.VMEM((tiles, AGR, chan), BF16),
            pltpu.VMEM((ha, patches), F32),
            pltpu.VMEM((patches, ha), BF16),
            pltpu.VMEM((tiles, agents, chan), BF16),
            pltpu.VMEM((tiles, 8, ha), F32),
            pltpu.VMEM((pieces, n_head - 1, 8, 128), F32),
            pltpu.VMEM((pieces, 8, 128), F32),
            dma((5,)), dma, dma, dma, dma, dma, dma, dma((pieces,)), dma((pieces,)), dma((8,)), dma((8,)),
        ],
        compiler_params=pltpu.CompilerParams(
            collective_id=0, has_side_effects=True, vmem_limit_bytes=need
        ),
        name="agent_attention",
    )(*[
        pltpu.with_memory_space_constraint(a, pltpu.HBM)
        for a in (queries, keys, values, positions.transpose(0, 2, 1), conv_weight)
    ])
    return pl.pallas_call(
        normalize,
        out_shape=jax.ShapeDtypeStruct(queries.shape, BF16),
        in_specs=[vmem, vmem, vmem, vmem],
        out_specs=hbm,
        scratch_shapes=[pltpu.VMEM((rows, cols, chan), BF16), dma((pieces,))],
        compiler_params=pltpu.CompilerParams(vmem_limit_bytes=8 * 1024 * 1024),
        name="normalize",
    )(summed, stats, gain.reshape(1, chan), bias.reshape(1, chan))


def solution(mesh):
    grid = P("row", "col", "head")
    in_specs = (grid, grid, grid, P(None, "row", "col"), P(None, "head"), P("head"), P("head"))
    body = functools.partial(shards, mesh.shape["row"], mesh.shape["col"], mesh.shape["head"])
    return jax.shard_map(body, mesh=mesh, in_specs=in_specs, out_specs=grid, check_vma=False)
```

profile of v0, /device:TPU:0, one launch (start us, length us, event | category | flops | bytes accessed | tf_op | source)
XLA Modules:
  0.0 19.6 jit_solution(6441527251210349794)
XLA Ops:
  0.0 0.0 copy-start.1
  0.0 0.0 copy-start
  0.0 18.4 %agent_attention.1 = (f32[48,32,256]{2,1,0:T(8,128)S(1)}, f32[3,8,128]{2,1,0:T(8,128)S(1)}) custom-call(bf16[48,32,256]{2,1,0:T(8,128)(2,1)} %q_hbm.1, bf16[48,32,256]{2,1,0:T(8,128)(2,1)} %k_hbm.1, bf16[48,32,256]{2,1,0:T(8,128)(2,1)} %v_hbm.1, s32[2,32,48]{2,1,0:T(8,128)} %bitcast.5, f32[9,256]{1,0:T(8,128)} %w_hbm.1), custom_call_target="tpu_custom_call" | custom-call | tf_op jit(solution)/shard_map/agent_attention/pallas_call | solution.py:334
  18.4 0.0 copy-done.1
  18.4 0.0 copy-done
  18.4 1.2 %normalize.1 = bf16[48,32,256]{2,1,0:T(8,128)(2,1)} custom-call(f32[48,32,256]{2,1,0:T(8,128)S(1)} %get-tuple-element.7.x_ref, f32[3,8,128]{2,1,0:T(8,128)S(1)} %get-tuple-element.8.stat_ref, f32[1,256]{1,0:T(1,128)S(1)} %bitcast.3, f32[1,256]{1,0:T(1,128)S(1)} %bitcast.4), custom_call_target="tpu_custom_call" | custom-call | tf_op jit(solution)/shard_map/normalize/pallas_call | solution.py:368
Async XLA Ops:
  0.0 18.4 %copy-start.1 = (f32[256]{0:T(256)S(1)}, f32[256]{0:T(256)}, u32[]{:S(2)}) copy-start(f32[256]{0:T(256)} %param.13) | copy-start | bytes 3076
  0.0 18.4 %copy-start = (f32[256]{0:T(256)S(1)}, f32[256]{0:T(256)}, u32[]{:S(2)}) copy-start(f32[256]{0:T(256)} %param.12) | copy-start | bytes 3076
where the time goes:
time: 19.8 us; the launch traced here: 19.6 us
  Pallas kernels  19.6 us (99%)
    pallas_call x1, Pallas kernels, shards(): pl.pallas_call(functools.partial(kernel, n_row, n_col, n_head), out_shape...  18.4 us
    pallas_call x1, Pallas kernels, shards(): pl.pallas_call(normalize, out_shape=jax.ShapeDtypeStruct(queries.shape, B...  1.21 us

commit v1 on v0

--- a/solution.py
+++ b/solution.py
@@ -21,6 +21,20 @@
 
 def iota(shape, dim):
     return lax.broadcasted_iota(jnp.int32, shape, dim)
+
+
+def cos_sin(x):
+    n = jnp.floor(x * (2.0 / math.pi) + 0.5)
+    r = ((x - n * 1.5703125) - n * 4.837512969970703125e-4) - n * 7.54978995489188216e-8
+    z = r * r
+    s = ((-1.9515295891e-4 * z + 8.3321608736e-3) * z - 1.6666654611e-1) * z * r + r
+    c = ((2.443315711809948e-5 * z - 1.388731625493765e-3) * z + 4.166664568298827e-2) * z * z
+    c = c - 0.5 * z + 1.0
+    quarter = n.astype(jnp.int32)
+    odd = (quarter & 1) == 1
+    cosine, sine = jnp.where(odd, s, c), jnp.where(odd, c, s)
+    cosine = jnp.where(((quarter + 1) & 2) == 2, -cosine, cosine)
+    return cosine, jnp.where((quarter & 2) == 2, -sine, sine)
 
 
 def kernel(
@@ -59,58 +73,83 @@
         pltpu.make_async_copy(v_hbm, vp.at[pl.ds(1, rows)], in_sem.at[2]),
         pltpu.make_async_copy(w_hbm, w_ref, in_sem.at[4]),
     ]
-    for c in loads:
+    for c in loads[:2]:
         c.start()
 
     barrier = pltpu.get_barrier_semaphore()
+    for o in range(1, n_head):
+        pl.semaphore_signal(barrier, inc=1, device_id=head_peer(o), device_id_type=MESH)
     for o in range(1, tiles):
         pl.semaphore_signal(barrier, inc=1, device_id=peer(o), device_id_type=MESH)
-    for o in range(1, n_head):
-        pl.semaphore_signal(barrier, inc=1, device_id=head_peer(o), device_id_type=MESH)
-
-    lane = iota((1, chan), 1)
-    freq = jnp.zeros((1, chan), F32)
+
+    step = rows // AGR
+    lead = -(-step // 8) * 8
+    bins, where = iota((lead + cols, step * cols), 0), iota((lead + cols, step * cols), 1)
+    pool = jnp.where(bins < lead, where // cols, where % cols + lead)
+    pool = (pool == bins).astype(BF16)
+
+    lane = iota((1, 128), 1)
+    freq = jnp.zeros((1, 128), F32)
     for j in range(HD // 4):
         freq = jnp.where(lane % (HD // 4) == j, F32(100.0 ** (-j / (HD // 4))), freq)
     row_lane = (lane % HD) < HD // 2
-    loads[0].wait()
-    eye = iota((rows, rows), 0) == iota((rows, rows), 1)
-    row_line = jnp.broadcast_to(pos_ref[0, 0:1, :].astype(F32), (rows, rows))
-    row_pos = jnp.sum(jnp.where(eye, row_line, 0.0), axis=1, keepdims=True)
-    col_pos = pos_ref[1, :, 0:1].astype(F32)
-    row_ang = row_pos * freq
-    col_ang = col_pos * freq
-    tabr[0] = jnp.where(row_lane, jnp.cos(row_ang), 0.0)
-    tabr[1] = jnp.where(row_lane, jnp.sin(row_ang), 0.0)
-    tabs[0] = jnp.where(row_lane, 0.0, jnp.cos(col_ang))
-    tabs[1] = jnp.where(row_lane, 0.0, jnp.sin(col_ang))
     src, dst = iota((chan, chan), 0), iota((chan, chan), 1)
     low = (dst % (HD // 2)) < HD // 4
     turn = jnp.where(low & (src - dst == HD // 4), -1.0, 0.0) + jnp.where(
         jnp.logical_not(low) & (dst - src == HD // 4), 1.0, 0.0
     )
     turn = turn.astype(BF16)
-
-    step = rows // AGR
+    loads[0].wait()
+    eye = iota((rows, rows), 0) == iota((rows, rows), 1)
+    row_line = jnp.broadcast_to(pos_ref[0, 0:1, :].astype(F32), (rows, rows))
+    row_pos = jnp.sum(jnp.where(eye, row_line, 0.0), axis=1, keepdims=True)
+    col_pos = pos_ref[1, :, 0:1].astype(F32)
+    longest = max(rows, cols)
+
+    def grow(x):
+        n = longest - x.shape[0]
+        return x if n == 0 else jnp.concatenate([x, jnp.zeros((n, 1), F32)], axis=0)
+
+    cosine, sine = cos_sin(jnp.where(row_lane, grow(row_pos), grow(col_pos)) * freq)
+    tabr[0] = jnp.where(row_lane, cosine[:rows], 0.0)
+    tabr[1] = jnp.where(row_lane, sine[:rows], 0.0)
+    tabs[0] = jnp.where(row_lane, 0.0, cosine[:cols])
+    tabs[1] = jnp.where(row_lane, 0.0, sine[:cols])
+
+    def wide(x):
+        return jnp.concatenate([x] * (chan // 128), axis=-1)
 
     def rotate(ref, to, cell):
         x = ref[pl.ds(cell * step, step)].reshape(step * cols, chan)
         crossed = jnp.dot(x, turn, preferred_element_type=F32).reshape(step, cols, chan)
         x = x.astype(F32).reshape(step, cols, chan)
-        cosine = tabr[0, pl.ds(cell * step, step)][:, None, :] + tabs[0][None]
-        sine = tabr[1, pl.ds(cell * step, step)][:, None, :] + tabs[1][None]
+        cosine = wide(tabr[0, pl.ds(cell * step, step)][:, None, :] + tabs[0][None])
+        sine = wide(tabr[1, pl.ds(cell * step, step)][:, None, :] + tabs[1][None])
         y = (x * cosine + crossed * sine).astype(BF16)
         to[pl.ds(cell * step * cols, step * cols)] = y.reshape(step * cols, chan)
-        return y
 
     loads[1].wait()
-    block = []
+    for c in loads[2:]:
+        c.start()
+    plain, across = [], []
     for cell in range(AGR):
-        y = rotate(q_in, qt, cell)
-        total = jnp.sum(y.astype(F32).reshape(step * cols, chan), axis=0, keepdims=True)
-        block.append((total * (1.0 / (step * cols))).astype(BF16).astype(F32))
-    block = jnp.concatenate(block, axis=0) * (1.0 / math.sqrt(HD))
-    ag[me] = block.astype(BF16)
+        x = q_in[pl.ds(cell * step, step)].reshape(step * cols, chan)
+        sums = jnp.dot(pool, x, preferred_element_type=F32)
+        for j, to in enumerate((plain, across)):
+            by_row = sums[:step] * wide(tabr[j, pl.ds(cell * step, step)])
+            by_col = sums[lead:] * wide(tabs[j])
+            to.append(
+                jnp.sum(by_row, axis=0, keepdims=True) + jnp.sum(by_col, axis=0, keepdims=True)
+            )
+    blank = [jnp.zeros((-AGR % 8, chan), F32)] if AGR % 8 else []
+    plain = jnp.concatenate(plain + blank, axis=0)
+    across = jnp.concatenate(across + blank, axis=0)
+    below = (iota(across.shape, 1) % (HD // 2)) < HD // 4
+    across = jnp.where(
+        below, -pltpu.roll(across, chan - HD // 4, 1), pltpu.roll(across, HD // 4, 1)
+    )
+    block = ((plain + across) * (1.0 / (step * cols))).astype(BF16).astype(F32)
+    ag[me] = (block * (1.0 / math.sqrt(HD)))[:AGR].astype(BF16)
 
     pl.semaphore_wait(barrier, tiles - 1 + n_head - 1)
     ag_copies = [
@@ -153,6 +192,8 @@
         def _():
             to[...] = jnp.zeros(to.shape, BF16)
 
+    for cell in range(AGR):
+        rotate(q_in, qt, cell)
     loads[2].wait()
     for cell in range(AGR):
         rotate(k_in, kt, cell)
@@ -198,8 +239,9 @@
     for c in merge:
         c.start()
 
-    for i in range(patches // chunk):
-        s = lax.dot_general(bd, qt[pl.ds(i * chunk, chunk)], NT, preferred_element_type=F32)
+    def query_softmax(i):
+        at = pl.ds(pl.multiple_of(i * chunk, chunk), chunk)
+        s = lax.dot_general(bd, qt[at], NT, preferred_element_type=F32)
         s = s.reshape(ha // 8, 8, chunk)
         m = jnp.max(s, axis=0)
         shift = heads
@@ -213,7 +255,16 @@
             z = z + pltpu.roll(z, shift, 0)
             shift *= 2
         p = (p * (1.0 / z)[None]).reshape(ha, chunk)
-        pt[pl.ds(i * chunk, chunk)] = p.T.astype(BF16)
+        pt[at] = p.T.astype(BF16)
+
+    batch = 3 if (patches // chunk) % 3 == 0 else 1
+
+    def query_batch(i, _):
+        for j in range(batch):
+            query_softmax(i * batch + j)
+        return 0
+
+    lax.fori_loop(0, patches // chunk // batch, query_batch, 0)
 
     for c, exists, comes in halos:
         pl.when(exists)(c.wait_send)
@@ -346,8 +397,8 @@
             pltpu.VMEM((rows + 2, 16, chan), BF16),
             pltpu.VMEM((patches, chan), BF16),
             pltpu.VMEM((patches, chan), BF16),
-            pltpu.VMEM((2, cols, chan), F32),
-            pltpu.VMEM((2, rows, chan), F32),
+            pltpu.VMEM((2, cols, 128), F32),
+            pltpu.VMEM((2, rows, 128), F32),
             pltpu.VMEM((tiles, AGR, chan), BF16),
             pltpu.VMEM((ha, patches), F32),
             pltpu.VMEM((patches, ha), BF16),

time: 19.8 us -> 19.7 us (level)
  no operation moved by 1% of the time
where the time goes in v1:
time: 19.7 us; the launch traced here: 19.6 us
  Pallas kernels  19.6 us (99%)
    pallas_call x1, Pallas kernels, shards(): pl.pallas_call(functools.partial(kernel, n_row, n_col, n_head), out_shape...  18.3 us
    pallas_call x1, Pallas kernels, shards(): pl.pallas_call(normalize, out_shape=jax.ShapeDtypeStruct(queries.shape, B...  1.21 us

profile of v1, /device:TPU:0, one launch (start us, length us, event | category | flops | bytes accessed | tf_op | source)
XLA Modules:
  0.0 19.6 jit_solution(12737196919963271793)
XLA Ops:
  0.0 0.0 copy-start.1
  0.0 0.0 copy-start
  0.0 18.3 %agent_attention.1 = (f32[48,32,256]{2,1,0:T(8,128)S(1)}, f32[3,8,128]{2,1,0:T(8,128)S(1)}) custom-call(bf16[48,32,256]{2,1,0:T(8,128)(2,1)} %q_hbm.1, bf16[48,32,256]{2,1,0:T(8,128)(2,1)} %k_hbm.1, bf16[48,32,256]{2,1,0:T(8,128)(2,1)} %v_hbm.1, s32[2,32,48]{2,1,0:T(8,128)} %bitcast.5, f32[9,256]{1,0:T(8,128)} %w_hbm.1), custom_call_target="tpu_custom_call" | custom-call | tf_op jit(solution)/shard_map/agent_attention/pallas_call | solution.py:385
  18.4 0.0 copy-done.1
  18.4 0.0 copy-done
  18.4 1.2 %normalize.1 = bf16[48,32,256]{2,1,0:T(8,128)(2,1)} custom-call(f32[48,32,256]{2,1,0:T(8,128)S(1)} %get-tuple-element.7.x_ref, f32[3,8,128]{2,1,0:T(8,128)S(1)} %get-tuple-element.8.stat_ref, f32[1,256]{1,0:T(1,128)S(1)} %bitcast.3, f32[1,256]{1,0:T(1,128)S(1)} %bitcast.4), custom_call_target="tpu_custom_call" | custom-call | tf_op jit(solution)/shard_map/normalize/pallas_call | solution.py:419
Async XLA Ops:
  0.0 18.4 %copy-start.1 = (f32[256]{0:T(256)S(1)}, f32[256]{0:T(256)}, u32[]{:S(2)}) copy-start(f32[256]{0:T(256)} %param.13) | copy-start | bytes 3076
  0.0 18.4 %copy-start = (f32[256]{0:T(256)S(1)}, f32[256]{0:T(256)}, u32[]{:S(2)}) copy-start(f32[256]{0:T(256)} %param.12) | copy-start | bytes 3076

commit v2 on v1

--- a/solution.py
+++ b/solution.py
@@ -12,6 +12,7 @@
 D = 1024
 AGR = 4
 EPS = 1e-05
+PIECE = 512
 F32 = jnp.float32
 BF16 = jnp.bfloat16
 MESH = pl.DeviceIdType.MESH
@@ -39,9 +40,9 @@
 
 def kernel(
     n_row, n_col, n_head,
-    q_hbm, k_hbm, v_hbm, pos_hbm, w_hbm,
-    conv, stat_ref,
-    pos_ref, w_ref, q_in, k_in, vp, lh, rh, qt, kt, tabs, tabr, ag, s_ref, pt, mb, sb, hb, own,
+    q_hbm, k_hbm, v_hbm, pos_hbm, w_hbm, gain_hbm, bias_hbm,
+    out, stat_ref,
+    conv, gain_ref, bias_ref, pos_ref, w_ref, q_in, k_in, vp, lh, rh, qt, kt, tabs, tabr, ag, s_ref, pt, mb, sb, hb, own,
     in_sem, ag_s, ag_r, mb_s, mb_r, sb_s, sb_r, hb_s, hb_r, halo_s, halo_r,
 ):
     rows, cols, chan = q_in.shape
@@ -66,21 +67,23 @@
             some, some, send, recv, device_id=peer(1), device_id_type=MESH
         )
 
+    barrier = pltpu.get_barrier_semaphore()
+    for o in range(1, tiles):
+        pl.semaphore_signal(barrier, inc=1, device_id=peer(o), device_id_type=MESH)
+    for o in range(1, n_head):
+        pl.semaphore_signal(barrier, inc=1, device_id=head_peer(o), device_id_type=MESH)
+
     loads = [
         pltpu.make_async_copy(pos_hbm, pos_ref, in_sem.at[3]),
         pltpu.make_async_copy(q_hbm, q_in, in_sem.at[0]),
         pltpu.make_async_copy(k_hbm, k_in, in_sem.at[1]),
         pltpu.make_async_copy(v_hbm, vp.at[pl.ds(1, rows)], in_sem.at[2]),
         pltpu.make_async_copy(w_hbm, w_ref, in_sem.at[4]),
+        pltpu.make_async_copy(gain_hbm, gain_ref, in_sem.at[5]),
+        pltpu.make_async_copy(bias_hbm, bias_ref, in_sem.at[6]),
     ]
     for c in loads[:2]:
         c.start()
-
-    barrier = pltpu.get_barrier_semaphore()
-    for o in range(1, n_head):
-        pl.semaphore_signal(barrier, inc=1, device_id=head_peer(o), device_id_type=MESH)
-    for o in range(1, tiles):
-        pl.semaphore_signal(barrier, inc=1, device_id=peer(o), device_id_type=MESH)
 
     step = rows // AGR
     lead = -(-step // 8) * 8
@@ -151,6 +154,8 @@
     block = ((plain + across) * (1.0 / (step * cols))).astype(BF16).astype(F32)
     ag[me] = (block * (1.0 / math.sqrt(HD)))[:AGR].astype(BF16)
 
+    for cell in range(AGR):
+        rotate(q_in, qt, cell)
     pl.semaphore_wait(barrier, tiles - 1 + n_head - 1)
     ag_copies = [
         pltpu.make_async_remote_copy(
@@ -192,8 +197,6 @@
         def _():
             to[...] = jnp.zeros(to.shape, BF16)
 
-    for cell in range(AGR):
-        rotate(q_in, qt, cell)
     loads[2].wait()
     for cell in range(AGR):
         rotate(k_in, kt, cell)
@@ -314,24 +317,35 @@
     blocks = size // 128
     lines = size // cols
     eye = iota((128, 128), 0) == iota((128, 128), 1)
+    ones = jnp.ones((16, chan), BF16)
+
+    def combine(p):
+        x = jnp.dot(pt[pl.ds(p * size, size)], av, preferred_element_type=F32)
+        x = (x + conv[pl.ds(p * lines, lines)].reshape(size, chan)).astype(BF16)
+        out[pl.ds(p * lines, lines)] = x.reshape(lines, cols, chan)
+        return x
+
+    later = combine(0)
     for p in range(pieces):
-        x = jnp.dot(pt[pl.ds(p * size, size)], av, preferred_element_type=F32)
-        x = x + conv[pl.ds(p * lines, lines)].reshape(size, chan)
-        conv[pl.ds(p * lines, lines)] = x.reshape(lines, cols, chan)
-        one = jnp.sum(x, axis=1, keepdims=True)
-        two = jnp.sum(x * x, axis=1, keepdims=True)
-        for j, what in enumerate((one, two)):
-            for b in range(blocks):
-                column = what[b * 128:(b + 1) * 128]
-                own[p, pl.ds(j * blocks + b, 1)] = jnp.sum(
-                    jnp.where(eye, column, 0.0), axis=0, keepdims=True
-                )
+        x = later
+        if p < pieces - 1:
+            later = combine(p + 1)
+        for b in range(blocks):
+            y = x[b * 128:(b + 1) * 128]
+            one = lax.dot_general(ones, y, NT, preferred_element_type=F32)
+            two = lax.dot_general(y, y, NT, preferred_element_type=F32)
+            own[p, pl.ds(b, 1)] = one[:1]
+            own[p, pl.ds(blocks + b, 1)] = jnp.sum(
+                jnp.where(eye, two, 0.0), axis=0, keepdims=True
+            )
         for o in range(1, n_head):
             pltpu.make_async_remote_copy(
                 own.at[p], hb.at[p, o - 1], hb_s.at[p], hb_r.at[p],
                 device_id=head_peer(o), device_id_type=MESH,
             ).start()
 
+    loads[5].wait()
+    loads[6].wait()
     for p in range(pieces):
         pltpu.make_async_remote_copy(
             hb.at[p], hb.at[p], hb_s.at[p], hb_r.at[p],
@@ -341,32 +355,39 @@
         for o in range(1, n_head):
             t = t + hb[p, o - 1]
         average = t[:blocks] * (1.0 / D)
-        variance = t[blocks:] * (1.0 / D) - average * average
-        stat_ref[p] = jnp.concatenate([average, lax.rsqrt(variance + EPS)], axis=0)
-
-
-def normalize(x_ref, stat_ref, gain_ref, bias_ref, out_hbm, obuf, out_sem):
-    rows, cols, chan = x_ref.shape
-    pieces = stat_ref.shape[0]
-    lines = rows // pieces
-    blocks = lines * cols // 128
+        variance = jnp.maximum(t[blocks:] * (1.0 / D) - average * average, 0.0)
+        stat_ref[...] = jnp.concatenate([average, lax.rsqrt(variance + EPS)], axis=0)
+        if p < pieces - 1:
+            normalize_piece(out, out, stat_ref, gain_ref[...], bias_ref[...], p * lines, p * lines)
+
+
+def normalize_piece(frm, to, stat_ref, gain, bias, start, put):
+    cols, chan = frm.shape[1:]
+    blocks = stat_ref.shape[0] // 2
     part = 128 // cols
-    gain, bias = gain_ref[...], bias_ref[...]
-    outs = []
-    for p in range(pieces):
-        for b in range(blocks):
-            a = jnp.broadcast_to(stat_ref[p, b:b + 1], (128, 128)).T
-            g = jnp.broadcast_to(stat_ref[p, blocks + b:blocks + b + 1], (128, 128)).T
-            a = jnp.concatenate([a] * (chan // 128), axis=1)
-            g = jnp.concatenate([g] * (chan // 128), axis=1)
-            at = pl.ds(p * lines + b * part, part)
-            y = (x_ref[at].reshape(128, chan) - a) * g * gain + bias
-            obuf[at] = y.astype(BF16).reshape(part, cols, chan)
-        at = pl.ds(p * lines, lines)
-        c = pltpu.make_async_copy(obuf.at[at], out_hbm.at[at], out_sem.at[p])
-        c.start()
-        outs.append(c)
-    for c in outs:
+    for b in range(blocks):
+        a = jnp.broadcast_to(stat_ref[b:b + 1], (128, 128)).T
+        g = jnp.broadcast_to(stat_ref[blocks + b:blocks + b + 1], (128, 128)).T
+        a = jnp.concatenate([a] * (chan // 128), axis=1)
+        g = jnp.concatenate([g] * (chan // 128), axis=1)
+        x = frm[pl.ds(start + b * part, part)].reshape(128, chan).astype(F32)
+        y = (x - a) * g * gain + bias
+        to[pl.ds(put + b * part, part)] = y.astype(BF16).reshape(part, cols, chan)
+
+
+def finish(x_ref, stat_ref, gain_ref, bias_ref, out_hbm, obuf, out_sem):
+    rows, lines = x_ref.shape[0], obuf.shape[0]
+    copies = []
+    if rows > lines:
+        at = pl.ds(0, rows - lines)
+        copies.append(pltpu.make_async_copy(x_ref.at[at], out_hbm.at[at], out_sem.at[0]))
+        copies[0].start()
+    normalize_piece(x_ref, obuf, stat_ref, gain_ref[...], bias_ref[...], rows - lines, 0)
+    copies.append(
+        pltpu.make_async_copy(obuf, out_hbm.at[pl.ds(rows - lines, lines)], out_sem.at[1])
+    )
+    copies[-1].start()
+    for c in copies:
         c.wait()
 
 
@@ -377,17 +398,21 @@
     agents = tiles * AGR
     ha = agents * heads
     patches = rows * cols
-    pieces = patches // 512
-    need = min(56 * 1024 * 1024, 14 * 1024 * 1024 + 4 * ha * tiles * agents * 8)
+    pieces = patches // PIECE
+    rest = 2 * PIECE // 128
+    need = min(56 * 1024 * 1024, 16 * 1024 * 1024 + 4 * ha * tiles * agents * 8)
     hbm = pl.BlockSpec(memory_space=pltpu.HBM)
     vmem = pl.BlockSpec(memory_space=pltpu.VMEM)
     dma = pltpu.SemaphoreType.DMA
     summed, stats = pl.pallas_call(
         functools.partial(kernel, n_row, n_col, n_head),
-        out_shape=[pltpu.VMEM((rows, cols, chan), F32), pltpu.VMEM((pieces, 8, 128), F32)],
-        in_specs=[hbm] * 5,
+        out_shape=[pltpu.VMEM((rows, cols, chan), BF16), pltpu.VMEM((rest, 128), F32)],
+        in_specs=[hbm] * 7,
         out_specs=[vmem, vmem],
         scratch_shapes=[
+            pltpu.VMEM((rows, cols, chan), F32),
+            pltpu.VMEM((1, chan), F32),
+            pltpu.VMEM((1, chan), F32),
             pltpu.VMEM((2, cols, rows), jnp.int32),
             pltpu.VMEM((9, chan), F32),
             pltpu.VMEM((rows, cols, chan), BF16),
@@ -404,9 +429,9 @@
             pltpu.VMEM((patches, ha), BF16),
             pltpu.VMEM((tiles, agents, chan), BF16),
             pltpu.VMEM((tiles, 8, ha), F32),
-            pltpu.VMEM((pieces, n_head - 1, 8, 128), F32),
-            pltpu.VMEM((pieces, 8, 128), F32),
-            dma((5,)), dma, dma, dma, dma, dma, dma, dma((pieces,)), dma((pieces,)), dma((8,)), dma((8,)),
+            pltpu.VMEM((pieces, n_head - 1, rest, 128), F32),
+            pltpu.VMEM((pieces, rest, 128), F32),
+            dma((7,)), dma, dma, dma, dma, dma, dma, dma((pieces,)), dma((pieces,)), dma((8,)), dma((8,)),
         ],
         compiler_params=pltpu.CompilerParams(
             collective_id=0, has_side_effects=True, vmem_limit_bytes=need
@@ -414,14 +439,17 @@
         name="agent_attention",
     )(*[
         pltpu.with_memory_space_constraint(a, pltpu.HBM)
-        for a in (queries, keys, values, positions.transpose(0, 2, 1), conv_weight)
+        for a in (
+            queries, keys, values, positions.transpose(0, 2, 1), conv_weight,
+            gain.reshape(1, chan), bias.reshape(1, chan),
+        )
     ])
     return pl.pallas_call(
-        normalize,
+        finish,
         out_shape=jax.ShapeDtypeStruct(queries.shape, BF16),
         in_specs=[vmem, vmem, vmem, vmem],
         out_specs=hbm,
-        scratch_shapes=[pltpu.VMEM((rows, cols, chan), BF16), dma((pieces,))],
+        scratch_shapes=[pltpu.VMEM((PIECE // cols, cols, chan), BF16), dma((2,))],
         compiler_params=pltpu.CompilerParams(vmem_limit_bytes=8 * 1024 * 1024),
         name="normalize",
     )(summed, stats, gain.reshape(1, chan), bias.reshape(1, chan))

time: 19.7 us -> 20 us (1.015)
  local copies, waits for them, and re-layouts: 0.01 us -> 0.67 us
  Pallas kernels: 19.6 us -> 19.2 us
    unnamed x4, local copies, waits for them, and re-layouts: 0.01 us -> 0.67 us
    pallas_call x1, Pallas kernels: 1.21 us -> 0.93 us  [shards(): pl.pallas_call(finish, out_shape=jax.ShapeDtypeStruct(queries.shape, BF16...]
where the time goes in v2:
time: 20 us; the launch traced here: 19.8 us
  Pallas kernels  19.2 us (96%)
  local copies, waits for them, and re-layouts  0.67 us (3%)
    pallas_call x1, Pallas kernels, shards(): pl.pallas_call(functools.partial(kernel, n_row, n_col, n_head), out_shape...  18.2 us
    pallas_call x1, Pallas kernels, shards(): pl.pallas_call(finish, out_shape=jax.ShapeDtypeStruct(queries.shape, BF16...  0.93 us
    unnamed x4, local copies, waits for them, and re-layouts  0.67 us

profile of v2, /device:TPU:0, one launch (start us, length us, event | category | flops | bytes accessed | tf_op | source)
XLA Modules:
  0.0 19.8 jit_solution(4844328847739525346)
XLA Ops:
  0.0 0.0 copy-start.1
  0.0 18.2 %agent_attention.1 = (bf16[48,32,256]{2,1,0:T(8,128)(2,1)S(1)}, f32[8,128]{1,0:T(8,128)S(1)}) custom-call(bf16[48,32,256]{2,1,0:T(8,128)(2,1)} %q_hbm.1, bf16[48,32,256]{2,1,0:T(8,128)(2,1)} %k_hbm.1, bf16[48,32,256]{2,1,0:T(8,128)(2,1)} %v_hbm.1, s32[2,32,48]{2,1,0:T(8,128)} %bitcast.7, f32[9,256]{1,0:T(8,128)} %w_hbm.1, f32[1,256]{1,0:T(1,128)} %bitcast.3, ...), custom_call_target="tpu_custom_call" | custom-call | tf_op jit(solution)/shard_map/agent_attention/pallas_call | solution.py:407
  18.2 0.0 copy-start
  18.2 0.0 copy-done.1
  18.3 0.7 %copy-done = f32[256]{0:T(256)S(1)} copy-done((f32[256]{0:T(256)S(1)}, f32[256]{0:T(256)}, u32[]{:S(2)}) %copy-start) | copy-done | bytes 1048
  18.9 0.9 %normalize.1 = bf16[48,32,256]{2,1,0:T(8,128)(2,1)} custom-call(bf16[48,32,256]{2,1,0:T(8,128)(2,1)S(1)} %get-tuple-element.7.x_ref, f32[8,128]{1,0:T(8,128)S(1)} %get-tuple-element.8.stat_ref, f32[1,256]{1,0:T(1,128)S(1)} %bitcast.4, f32[1,256]{1,0:T(1,128)S(1)} %bitcast.6), custom_call_target="tpu_custom_call" | custom-call | tf_op jit(solution)/shard_map/normalize/pallas_call | solution.py:447
Async XLA Ops:
  0.0 18.3 %copy-start.1 = (f32[256]{0:T(256)S(1)}, f32[256]{0:T(256)}, u32[]{:S(2)}) copy-start(f32[256]{0:T(256)} %param.13) | copy-start | bytes 3076
  18.2 0.7 %copy-start = (f32[256]{0:T(256)S(1)}, f32[256]{0:T(256)}, u32[]{:S(2)}) copy-start(f32[256]{0:T(256)} %param.12) | copy-start | bytes 3076

commit v3 on v2

--- a/solution.py
+++ b/solution.py
@@ -41,7 +41,7 @@
 def kernel(
     n_row, n_col, n_head,
     q_hbm, k_hbm, v_hbm, pos_hbm, w_hbm, gain_hbm, bias_hbm,
-    out, stat_ref,
+    out, stat_ref, affine,
     conv, gain_ref, bias_ref, pos_ref, w_ref, q_in, k_in, vp, lh, rh, qt, kt, tabs, tabr, ag, s_ref, pt, mb, sb, hb, own,
     in_sem, ag_s, ag_r, mb_s, mb_r, sb_s, sb_r, hb_s, hb_r, halo_s, halo_r,
 ):
@@ -332,11 +332,12 @@
             later = combine(p + 1)
         for b in range(blocks):
             y = x[b * 128:(b + 1) * 128]
-            one = lax.dot_general(ones, y, NT, preferred_element_type=F32)
-            two = lax.dot_general(y, y, NT, preferred_element_type=F32)
-            own[p, pl.ds(b, 1)] = one[:1]
+            both = lax.dot_general(
+                jnp.concatenate([ones, y], axis=0), y, NT, preferred_element_type=F32
+            )
+            own[p, pl.ds(b, 1)] = both[:1]
             own[p, pl.ds(blocks + b, 1)] = jnp.sum(
-                jnp.where(eye, two, 0.0), axis=0, keepdims=True
+                jnp.where(eye, both[16:], 0.0), axis=0, keepdims=True
             )
         for o in range(1, n_head):
             pltpu.make_async_remote_copy(
@@ -346,6 +347,8 @@
 
     loads[5].wait()
     loads[6].wait()
+    affine[0:1] = gain_ref[...]
+    affine[1:2] = bias_ref[...]
     for p in range(pieces):
         pltpu.make_async_remote_copy(
             hb.at[p], hb.at[p], hb_s.at[p], hb_r.at[p],
@@ -375,14 +378,14 @@
         to[pl.ds(put + b * part, part)] = y.astype(BF16).reshape(part, cols, chan)
 
 
-def finish(x_ref, stat_ref, gain_ref, bias_ref, out_hbm, obuf, out_sem):
+def finish(x_ref, stat_ref, affine, out_hbm, obuf, out_sem):
     rows, lines = x_ref.shape[0], obuf.shape[0]
     copies = []
     if rows > lines:
         at = pl.ds(0, rows - lines)
         copies.append(pltpu.make_async_copy(x_ref.at[at], out_hbm.at[at], out_sem.at[0]))
         copies[0].start()
-    normalize_piece(x_ref, obuf, stat_ref, gain_ref[...], bias_ref[...], rows - lines, 0)
+    normalize_piece(x_ref, obuf, stat_ref, affine[0:1], affine[1:2], rows - lines, 0)
     copies.append(
         pltpu.make_async_copy(obuf, out_hbm.at[pl.ds(rows - lines, lines)], out_sem.at[1])
     )
@@ -404,11 +407,11 @@
     hbm = pl.BlockSpec(memory_space=pltpu.HBM)
     vmem = pl.BlockSpec(memory_space=pltpu.VMEM)
     dma = pltpu.SemaphoreType.DMA
-    summed, stats = pl.pallas_call(
+    summed, stats, affine = pl.pallas_call(
         functools.partial(kernel, n_row, n_col, n_head),
-        out_shape=[pltpu.VMEM((rows, cols, chan), BF16), pltpu.VMEM((rest, 128), F32)],
+        out_shape=[pltpu.VMEM((rows, cols, chan), BF16), pltpu.VMEM((rest, 128), F32), pltpu.VMEM((2, chan), F32)],
         in_specs=[hbm] * 7,
-        out_specs=[vmem, vmem],
+        out_specs=[vmem, vmem, vmem],
         scratch_shapes=[
             pltpu.VMEM((rows, cols, chan), F32),
             pltpu.VMEM((1, chan), F32),
@@ -447,12 +450,12 @@
     return pl.pallas_call(
         finish,
         out_shape=jax.ShapeDtypeStruct(queries.shape, BF16),
-        in_specs=[vmem, vmem, vmem, vmem],
+        in_specs=[vmem, vmem, vmem],
         out_specs=hbm,
         scratch_shapes=[pltpu.VMEM((PIECE // cols, cols, chan), BF16), dma((2,))],
         compiler_params=pltpu.CompilerParams(vmem_limit_bytes=8 * 1024 * 1024),
         name="normalize",
-    )(summed, stats, gain.reshape(1, chan), bias.reshape(1, chan))
+    )(summed, stats, affine)
 
 
 def solution(mesh):

time: 20 us -> 19.2 us (0.960)
  local copies, waits for them, and re-layouts: 0.67 us -> 0 us
    unnamed x4 -> x0, local copies, waits for them, and re-layouts: 0.67 us -> none
where the time goes in v3:
time: 19.2 us; the launch traced here: 19.1 us
  Pallas kernels  19.1 us (99%)
    pallas_call x1, Pallas kernels, shards(): pl.pallas_call(functools.partial(kernel, n_row, n_col, n_head), out_shape...  18.1 us
    pallas_call x1, Pallas kernels, shards(): pl.pallas_call(finish, out_shape=jax.ShapeDtypeStruct(queries.shape, BF16...  0.93 us

profile of v3, /device:TPU:0, one launch (start us, length us, event | category | flops | bytes accessed | tf_op | source)
XLA Modules:
  0.0 19.1 jit_solution(11067676233212202559)
XLA Ops:
  0.0 18.1 %agent_attention.1 = (bf16[48,32,256]{2,1,0:T(8,128)(2,1)S(1)}, f32[8,128]{1,0:T(8,128)S(1)}, f32[2,256]{1,0:T(2,128)S(1)}) custom-call(bf16[48,32,256]{2,1,0:T(8,128)(2,1)} %q_hbm.1, bf16[48,32,256]{2,1,0:T(8,128)(2,1)} %k_hbm.1, bf16[48,32,256]{2,1,0:T(8,128)(2,1)} %v_hbm.1, s32[2,32,48]{2,1,0:T(8,128)} %bitcast.3, f32[9,256]{1,0:T(8,128)} %w_hbm.1, ...), custom_call_target="tpu_custom_call" | custom-call | tf_op jit(solution)/shard_map/agent_attention/pallas_call | solution.py:410
  18.2 0.9 %normalize.1 = bf16[48,32,256]{2,1,0:T(8,128)(2,1)} custom-call(bf16[48,32,256]{2,1,0:T(8,128)(2,1)S(1)} %get-tuple-element.8.x_ref, f32[8,128]{1,0:T(8,128)S(1)} %get-tuple-element.9.stat_ref, f32[2,256]{1,0:T(2,128)S(1)} %get-tuple-element.10.affine), custom_call_target="tpu_custom_call" | custom-call | tf_op jit(solution)/shard_map/normalize/pallas_call | solution.py:450
